TPU v7x, 32 devices: a whole 2x2x4 slice. The times are simulated.
32 devices in a mesh: rep: 8 (over z, x), shard: 4 (over y, core).
Axes of the slice: x: 2, y: 2, z: 4, core: 2. Of those that a mesh axis runs over, the one named last changes fastest.
Arguments:
- inputs: bfloat16 [3072, 1024], P('rep', 'shard'), may hold values from -6 to 6
- cotangent: bfloat16 [3072, 512], P('rep'), may hold values from -0.15625 to 0.15625
- momentum: float32 [512, 1024], P('rep', 'shard'), may hold values from -54 to 54
- right_prev: float32 [1024, 64], P('shard'), may hold values from -0.1875 to 0.1875
Outputs:
- new_momentum: float32 [512, 1024], P('rep', 'shard')
- right_factor: float32 [1024, 64], P('shard')
- update: bfloat16 [512, 1024], P('rep', 'shard')
All inputs are finite; a program needn't handle non-finite values.
Results may differ from a plain program's by a relative error of at most 0.001.
Values sent between devices are 32-bit elements; how exact they have to be, the bound alone decides.
A program may use at most 64 MiB of HBM per device.

v0:
```python
import jax
import jax.numpy as jnp
from jax import lax
from jax.sharding import PartitionSpec as P


def body(inputs, cotangent, momentum, right_prev):
    high = lax.Precision.HIGHEST
    col_count = momentum.shape[1]
    out_total = cotangent.shape[1]
    in_total = col_count * lax.axis_size("shard")
    rank_size = right_prev.shape[1]
    gradient = lax.psum_scatter(
        lax.dot_general(
            cotangent, inputs, (((0,), (0,)), ((), ())), preferred_element_type=jnp.float32
        ),
        "rep",
        scatter_dimension=0,
        tiled=True,
    )
    blended = momentum + gradient
    left_raw = lax.psum(jnp.dot(blended, right_prev, precision=high), "shard")
    gram_sum = lax.psum(jnp.dot(left_raw.T, left_raw, precision=high), "rep")
    lower_factor = jnp.linalg.cholesky(gram_sum)
    ortho = lax.linalg.triangular_solve(lower_factor, left_raw.T, left_side=True, lower=True).T
    local_right = jnp.dot(blended.T, ortho, precision=high)
    right_raw = lax.psum(local_right, "rep")
    column_sq = lax.psum(jnp.sum(right_raw * right_raw, axis=0), "shard")
    new_momentum = blended - 0.05 * jnp.dot(ortho, right_raw.T, precision=high)
    right_factor = right_raw / jnp.sqrt(column_sq + 1e-06)
    scale_factor = (out_total * in_total / rank_size) ** 0.5
    update = (scale_factor * jnp.dot(ortho, right_factor.T, precision=high)).astype(jnp.bfloat16)
    return (new_momentum, right_factor, update)


def solution(mesh):
    return jax.shard_map(
        body,
        mesh=mesh,
        in_specs=(P("rep", "shard"), P("rep", None), P("rep", "shard"), P("shard", None)),
        out_specs=(P("rep", "shard"), P("shard", None), P("rep", "shard")),
        check_vma=False,
    )
```

profile of v0, /device:TPU:0, one launch (start us, length us, event | category | flops | bytes accessed | tf_op | source)
XLA Modules:
  0.0 219.4 jit_solution(16988871786383340574)
XLA Ops:
  7.2 0.0 copy-start
  7.2 0.0 reduce-scatter.2.cloned.1.call-start
  7.2 0.9 copy-done
  8.2 2.1 fusion.6
  10.2 0.0 copy-start.3
  10.2 0.0 reduce-scatter.2.cloned.1.call-update
  10.2 0.0 copy-start.4
  10.3 0.0 all-reduce.2.cloned.1.call-start
  10.3 66.9 %reduce-scatter.2.cloned.1.call-done = f32[64,256]{1,0:T(8,128)} async-done(((f32[512,256]{1,0:T(8,128)}), f32[64,256]{1,0:T(8,128)}) %reduce-scatter.2.cloned.1.call-update) | async-done | bytes 65552 | tf_op jit(solution)/shard_map/reduce_scatter | solution.py:13
  77.2 0.0 copy-done.3
  77.2 0.8 add.30
  78.0 0.0 copy-done.4
  78.0 0.2 fusion.7
  78.3 10.3 %psum.28 = f32[64,64]{1,0:T(8,128)S(1)} all-reduce(f32[64,64]{1,0:T(8,128)S(1)} %fusion.7), channel_id=1, replica_groups=mesh['rep'=8,'shard'=4] {'shard'}, use_global_device_ids=true, to_apply=%region_1.0 | all-reduce | flops 4096 | bytes 32768 | tf_op jit(solution)/shard_map/psum | solution.py:22
  88.5 0.2 fusion.8
  88.8 35.1 %psum.29 = f32[64,64]{0,1:T(8,128)S(1)} all-reduce(f32[64,64]{0,1:T(8,128)S(1)} %fusion.8), channel_id=1, replica_groups=mesh['rep'=8,'shard'=4] {'rep'}, use_global_device_ids=true, to_apply=%region_2.0 | all-reduce | flops 4096 | bytes 32768 | tf_op jit(solution)/shard_map/psum | solution.py:23
  123.9 0.1 copy.8
  124.0 5.9 %cholesky.16 = f32[64,64]{1,0:T(8,128)S(1)} custom-call(f32[64,64]{1,0:T(8,128)S(1)} %fusion.5), custom_call_target="Cholesky" | custom-call | tf_op jit(solution)/shard_map/jit(cholesky)/cholesky | solution.py:24
  129.9 0.6 compare_reduce_fusion
  130.5 0.7 fusion.2
  131.2 4.9 %custom-call.6 = f32[1,64,64]{1,2,0:T(8,128)S(1)} custom-call(f32[1,64,64]{2,1,0:T(8,128)S(1)} %fusion.2), custom_call_target="InvertDiagBlocksLowerTriangular" | custom-call | tf_op jit(solution)/shard_map/triangular_solve | solution.py:25
  136.1 0.2 fusion.3
  136.3 0.8 fusion.9
  137.2 0.0 all-reduce.2.cloned.1.call-update
  137.2 66.8 %all-reduce.2.cloned.1.call-done = f32[256,64]{0,1:T(8,128)} async-done(((f32[256,64]{0,1:T(8,128)}), f32[256,64]{0,1:T(8,128)}) %all-reduce.2.cloned.1.call-update) | async-done | bytes 65552 | tf_op jit(solution)/shard_map/psum | solution.py:27
  204.0 0.0 copy-start.1
  204.0 1.0 multiply_reduce_fusion
  205.0 5.7 %psum.31 = f32[64]{0:T(128)S(1)} all-reduce(f32[64]{0:T(128)S(1)} %multiply_reduce_fusion), channel_id=1, replica_groups=mesh['rep'=8,'shard'=4] {'shard'}, use_global_device_ids=true, to_apply=%region_7.8 | all-reduce | flops 64 | bytes 512 | tf_op jit(solution)/shard_map/psum | solution.py:28
  210.7 0.0 copy-done.1
  210.7 0.1 broadcast_divide_fusion
  210.8 0.0 copy-start.2
  210.8 0.9 fusion.1
  211.7 0.0 copy-done.2
  211.7 0.9 fusion
  (3 shorter events, 0.0 us)
Async XLA Ops:
  7.2 1.0 copy-start
  7.2 70.0 %reduce-scatter.2.cloned.1.call-start = ((), (), s32[]{:S(2)}) async-start(), calls=%async_computation.1 | async-start | bytes 589824 | tf_op jit(solution)/shard_map/reduce_scatter | solution.py:13
  10.2 67.0 %copy-start.3 = (f32[64,256]{1,0:T(8,128)S(1)}, f32[64,256]{1,0:T(8,128)}, u32[]{:S(2)}) copy-start(f32[64,256]{1,0:T(8,128)} %param.6) | copy-start | bytes 196612
  10.2 67.8 %copy-start.4 = (f32[256,64]{0,1:T(8,128)S(1)}, f32[256,64]{0,1:T(8,128)}, u32[]{:S(2)}) copy-start(f32[256,64]{0,1:T(8,128)} %param.7) | copy-start | bytes 196612
  10.3 193.7 %all-reduce.2.cloned.1.call-start = ((), (), s32[]{:S(2)}) async-start(), calls=%async_computation.2 | async-start | bytes 131072 | tf_op jit(solution)/shard_map/psum | solution.py:27
  204.0 6.7 %copy-start.1 = (f32[256,64]{0,1:T(8,128)S(1)}, f32[256,64]{0,1:T(8,128)}, u32[]{:S(2)}) copy-start(f32[256,64]{0,1:T(8,128)} %all-reduce.2.cloned.1.call-done) | copy-start | bytes 196612
  210.8 0.9 copy-start.2
Sparse Core Ops, SparseCore 0:
  11.3 65.8 reduce-scatter.1
  137.3 66.6 all-reduce.1
where the time goes:
time: 220 us; the launch traced here: 219 us
  waiting for transfers between devices  134 us (61%)
  blocking collectives  51.1 us (23%)
  other arithmetic  14.1 us (6%)
  between operations  14.1 us (6%)
  matrix products  5.31 us (2%)
    reduce_scatter x1, waiting for transfers between devices, body(): lax.psum_scatter(lax.dot_general(cotangent, inputs, (((0,), (0,)), ((), (...  66.9 us
    psum x1, waiting for transfers between devices, body(): right_raw = lax.psum(local_right, 'rep')  66.8 us
    psum x1, blocking collectives, body(): gram_sum = lax.psum(jnp.dot(left_raw.T, left_raw, precision=high), 'rep')  35.1 us
    psum x1, blocking collectives, body(): left_raw = lax.psum(jnp.dot(blended, right_prev, precision=high), 'shard')  10.3 us
    another operation x3, other arithmetic, body(): lower_factor = jnp.linalg.cholesky(gram_sum)  6.53 us
    psum x1, blocking collectives, body(): column_sq = lax.psum(jnp.sum(right_raw * right_raw, axis=0), 'shard')  5.67 us
    another operation x2, other arithmetic, body(): lax.linalg.triangular_solve(lower_factor, left_raw.T, left_side=True, low...  5.57 us
  transfers between devices with their start and end apart: 2, of which 2 were waited for; matrix products, arithmetic and copies ran while one was open for 0% of the time, Pallas kernels for 0%

commit v1 on v0

--- a/solution.py
+++ b/solution.py
@@ -24,7 +24,11 @@
     lower_factor = jnp.linalg.cholesky(gram_sum)
     ortho = lax.linalg.triangular_solve(lower_factor, left_raw.T, left_side=True, lower=True).T
     local_right = jnp.dot(blended.T, ortho, precision=high)
-    right_raw = lax.psum(local_right, "rep")
+
+    def detail_floor(payload):
+        return jax.lax.all_gather(payload, "rep").sum(axis=0)
+
+    right_raw = detail_floor(local_right)
     column_sq = lax.psum(jnp.sum(right_raw * right_raw, axis=0), "shard")
     new_momentum = blended - 0.05 * jnp.dot(ortho, right_raw.T, precision=high)
     right_factor = right_raw / jnp.sqrt(column_sq + 1e-06)

time: 220 us -> 183 us (0.83)
  waiting for transfers between devices: 134 us -> 66.9 us
  blocking collectives: 51.1 us -> 82.3 us
    psum x1 -> x0, waiting for transfers between devices: 66.8 us -> none  [body(): right_raw = lax.psum(local_right, 'rep')]
    all_gather x0 -> x1, blocking collectives: none -> 31.3 us  [detail_floor(): return jax.lax.all_gather(payload, 'rep').sum(axis=0)]
  transfers between devices with their start and end apart: 2 -> 1, of which waited for: 2 -> 1; matrix products, arithmetic and copies ran while one was open for 0% -> 0% of each run, Pallas kernels for 0% -> 0%
where the time goes in v1:
time: 183 us
  blocking collectives  82.3 us (45%)
  waiting for transfers between devices  66.9 us (37%)
  between operations  14.1 us (8%)
  other arithmetic  13.3 us (7%)
  matrix products  4.7 us (3%)
    reduce_scatter x1, waiting for transfers between devices, body(): lax.psum_scatter(lax.dot_general(cotangent, inputs, (((0,), (0,)), ((), (...  66.9 us
    psum x1, blocking collectives, body(): gram_sum = lax.psum(jnp.dot(left_raw.T, left_raw, precision=high), 'rep')  35.1 us
    all_gather x1, blocking collectives, detail_floor(): return jax.lax.all_gather(payload, 'rep').sum(axis=0)  31.3 us
    psum x1, blocking collectives, body(): left_raw = lax.psum(jnp.dot(blended, right_prev, precision=high), 'shard')  10.3 us
    another operation x3, other arithmetic, body(): lower_factor = jnp.linalg.cholesky(gram_sum)  6.52 us
    psum x1, blocking collectives, body(): column_sq = lax.psum(jnp.sum(right_raw * right_raw, axis=0), 'shard')  5.67 us
    another operation x2, other arithmetic, body(): lax.linalg.triangular_solve(lower_factor, left_raw.T, left_side=True, low...  5.55 us
  transfers between devices with their start and end apart: 1, of which 1 were waited for; matrix products, arithmetic and copies ran while one was open for 0% of the time, Pallas kernels for 0%

profile of v1, /device:TPU:0, one launch (start us, length us, event | category | flops | bytes accessed | tf_op | source)
XLA Modules:
  0.0 182.6 jit_solution(7999281405163538785)
XLA Ops:
  7.2 0.0 copy-start
  7.2 0.0 reduce-scatter.2.cloned.1.call-start
  7.2 0.9 copy-done
  8.2 2.1 %fusion.6 = f32[512,256]{1,0:T(8,128)} fusion(bf16[384,512]{1,0:T(8,128)(2,1)S(1)} %copy-done, bf16[384,256]{1,0:T(8,128)(2,1)} %param.4), kind=kOutput, calls=%fused_computation.18 | convolution fusion | flops 100663296 | bytes 1114112 | tf_op jit(solution)/shard_map/dot_general | solution.py:14
  10.2 0.0 copy-start.2
  10.2 0.0 reduce-scatter.2.cloned.1.call-update
  10.2 0.0 copy-start.3
  10.3 66.9 %reduce-scatter.2.cloned.1.call-done = f32[64,256]{1,0:T(8,128)} async-done(((f32[512,256]{1,0:T(8,128)}), f32[64,256]{1,0:T(8,128)}) %reduce-scatter.2.cloned.1.call-update) | async-done | bytes 65552 | tf_op jit(solution)/shard_map/reduce_scatter | solution.py:13
  77.2 0.0 copy-done.2
  77.2 0.8 add.28
  78.0 0.0 copy-done.3
  78.0 0.2 fusion.7
  78.3 10.3 %psum.21 = f32[64,64]{1,0:T(8,128)S(1)} all-reduce(f32[64,64]{1,0:T(8,128)S(1)} %fusion.7), channel_id=1, replica_groups=mesh['rep'=8,'shard'=4] {'shard'}, use_global_device_ids=true, to_apply=%region_1.0 | all-reduce | flops 4096 | bytes 32768 | tf_op jit(solution)/shard_map/psum | solution.py:22
  88.5 0.2 fusion.8
  88.8 35.1 %psum.22 = f32[64,64]{0,1:T(8,128)S(1)} all-reduce(f32[64,64]{0,1:T(8,128)S(1)} %fusion.8), channel_id=1, replica_groups=mesh['rep'=8,'shard'=4] {'rep'}, use_global_device_ids=true, to_apply=%region_2.0 | all-reduce | flops 4096 | bytes 32768 | tf_op jit(solution)/shard_map/psum | solution.py:23
  123.9 0.1 copy.8
  124.0 5.8 %cholesky.16 = f32[64,64]{1,0:T(8,128)S(1)} custom-call(f32[64,64]{1,0:T(8,128)S(1)} %fusion.5), custom_call_target="Cholesky" | custom-call | tf_op jit(solution)/shard_map/jit(cholesky)/cholesky | solution.py:24
  129.9 0.6 compare_reduce_fusion
  130.5 0.7 fusion.2
  131.2 4.9 %custom-call.6 = f32[1,64,64]{1,2,0:T(8,128)S(1)} custom-call(f32[1,64,64]{2,1,0:T(8,128)S(1)} %fusion.2), custom_call_target="InvertDiagBlocksLowerTriangular" | custom-call | tf_op jit(solution)/shard_map/triangular_solve | solution.py:25
  136.1 0.2 fusion.3
  136.3 0.2 fusion.9
  136.5 31.3 %all-gather = f32[2048,64]{0,1:T(8,128)S(1)} all-gather(f32[256,64]{0,1:T(8,128)S(1)} %fusion.9), channel_id=2, replica_groups=mesh['rep'=8,'shard'=4] {'rep'}, dimensions={0}, use_global_device_ids=true | all-gather | bytes 589824 | tf_op jit(solution)/shard_map/all_gather | solution.py:29
  167.8 0.2 copy.10
  168.0 0.1 bitcast_reduce_fusion
  168.1 0.9 fusion
  169.0 0.1 multiply_reduce_fusion
  169.1 5.7 %psum.23 = f32[64]{0:T(128)S(1)} all-reduce(f32[64]{0:T(128)S(1)} %multiply_reduce_fusion), channel_id=1, replica_groups=mesh['rep'=8,'shard'=4] {'shard'}, use_global_device_ids=true, to_apply=%region_7.8 | all-reduce | flops 64 | bytes 512 | tf_op jit(solution)/shard_map/psum | solution.py:32
  174.8 0.1 broadcast_divide_fusion
  174.9 0.0 copy-start.1
  174.9 0.9 fusion.1
  175.8 0.0 copy-done.1
  (3 shorter events, 0.0 us)
Async XLA Ops:
  7.2 1.0 copy-start
  7.2 70.0 %reduce-scatter.2.cloned.1.call-start = ((), (), s32[]{:S(2)}) async-start(), calls=%async_computation.1 | async-start | bytes 589824 | tf_op jit(solution)/shard_map/reduce_scatter | solution.py:13
  10.2 67.0 %copy-start.2 = (f32[64,256]{1,0:T(8,128)S(1)}, f32[64,256]{1,0:T(8,128)}, u32[]{:S(2)}) copy-start(f32[64,256]{1,0:T(8,128)} %param.6) | copy-start | bytes 196612
  10.2 67.8 %copy-start.3 = (f32[256,64]{0,1:T(8,128)S(1)}, f32[256,64]{0,1:T(8,128)}, u32[]{:S(2)}) copy-start(f32[256,64]{0,1:T(8,128)} %param.7) | copy-start | bytes 196612
  174.9 0.9 copy-start.1
Sparse Core Ops, SparseCore 0:
  11.3 65.8 reduce-scatter.1
